TPU v7x, 256 devices: a whole 4x4x8 slice. The times are simulated.
256 devices in a mesh: row: 32 (over z, y), col: 8 (over x, core).
Axes of the slice: x: 4, y: 4, z: 8, core: 2. Of those that a mesh axis runs over, the one named last changes fastest.
Arguments:
- inputs: bfloat16 [16384, 2048], P('row', 'col'), may hold values from -6 to 6
- grad_out: bfloat16 [16384, 2048], P('row', 'col'), may hold values from -6 to 6
- gate_pre: bfloat16 [16384, 7168], P('row', 'col'), may hold values from -8 to 8
- up_pre: bfloat16 [16384, 7168], P('row', 'col'), may hold values from -6 to 6
- gate_weight: bfloat16 [2048, 7168], P('row', 'col'), may hold values from -0.125 to 0.125
- up_weight: bfloat16 [2048, 7168], P('row', 'col'), may hold values from -0.125 to 0.125
- down_weight: bfloat16 [2048, 7168], P('row', 'col'), may hold values from -0.125 to 0.125
Outputs:
- d_inputs: bfloat16 [16384, 2048], P('row', 'col')
- gate_grad: bfloat16 [2048, 7168], P('row', 'col')
- up_grad: bfloat16 [2048, 7168], P('row', 'col')
- down_grad: bfloat16 [2048, 7168], P('row', 'col')
All inputs are finite; a program needn't handle non-finite values.
Results may differ from a plain program's by a relative error of at most 0.015.
Values may be sent and summed in bfloat16 or wider, within the bound.
No kernel may reach another device: no remote copies, remote signals or barrier semaphores. Data moves between devices by JAX's collectives and lax.ppermute only.
A program may use at most 128 MiB of HBM per device.

v0:
```python
import math
import jax
import jax.numpy as jnp
from jax import lax
from jax.sharding import PartitionSpec as P


def against(left, right):
    return lax.dot_general(
        left, right, (((1,), (1,)), ((), ())), preferred_element_type=jnp.float32
    )


def body(inputs, grad_out, gate_pre, up_pre, gate_weight, up_weight, down_weight):
    rows_here = grad_out.shape[0]
    hidden_here = gate_pre.shape[1]
    factor = 1.0 / math.sqrt(rows_here * lax.axis_size("row"))
    full_inputs, full_grads = (
        lax.all_gather(inputs, "col", axis=1, tiled=True),
        lax.all_gather(grad_out, "col", axis=1, tiled=True),
    )
    d_hidden = jnp.dot(
        full_grads,
        lax.all_gather(down_weight, "row", axis=0, tiled=True),
        preferred_element_type=jnp.float32,
    )
    gate_vals = gate_pre.astype(jnp.float32)
    up_vals = up_pre.astype(jnp.float32)
    sigma = jax.nn.sigmoid(gate_vals)
    active = gate_vals * sigma
    hidden = (active * up_vals).astype(jnp.bfloat16)
    d_gate = (d_hidden * up_vals * sigma * (1.0 + gate_vals * (1.0 - sigma))).astype(jnp.bfloat16)
    d_up = (d_hidden * active).astype(jnp.bfloat16)

    def grad_term(left, right):
        product = lax.dot_general(
            left, right, (((0,), (0,)), ((), ())), preferred_element_type=jnp.float32
        )
        return product * factor

    down_grad = lax.psum_scatter(
        grad_term(full_grads, hidden).astype(jnp.bfloat16), "row", scatter_dimension=0, tiled=True
    )
    part = against(d_gate, lax.all_gather(gate_weight, "row", axis=0, tiled=True)) + against(
        d_up, lax.all_gather(up_weight, "row", axis=0, tiled=True)
    )
    d_inputs = lax.psum_scatter(part.astype(jnp.bfloat16), "col", scatter_dimension=1, tiled=True)
    paired = lax.psum_scatter(
        jnp.concatenate(
            [grad_term(full_inputs, d_gate), grad_term(full_inputs, d_up)], axis=1
        ).astype(jnp.bfloat16),
        "row",
        scatter_dimension=0,
        tiled=True,
    ).astype(jnp.float32)
    gate_grad = paired[:, :hidden_here].astype(jnp.bfloat16)
    up_grad = paired[:, hidden_here:].astype(jnp.bfloat16)
    return (d_inputs, gate_grad, up_grad, down_grad)


def solution(mesh):
    in_specs = (
        P("row", "col"),
        P("row", "col"),
        P("row", "col"),
        P("row", "col"),
        P("row", "col"),
        P("row", "col"),
        P("row", "col"),
    )
    out_specs = (P("row", "col"), P("row", "col"), P("row", "col"), P("row", "col"))
    return jax.shard_map(body, mesh=mesh, in_specs=in_specs, out_specs=out_specs, check_vma=False)
```

profile of v0, /device:TPU:8, one launch (start us, length us, event | category | flops | bytes accessed | tf_op | source)
XLA Modules:
  0.0 815.9 jit_solution(1968349745473048420)
XLA Ops:
  7.2 0.0 all-gather.6.cloned.1.call-start
  7.2 0.7 all-gather.6.cloned.1.call-update
  7.9 0.0 all-gather.8.cloned.1.call-start
  7.9 0.7 all-gather.8.cloned.1.call-update
  8.6 0.0 all-gather.14.cloned.1.call-start
  8.7 0.7 all-gather.14.cloned.1.call-update
  9.4 0.0 all-gather.10.cloned.1.call-start
  9.4 0.5 all-gather.10.cloned.1.call-update
  10.0 0.0 all-gather.12.cloned.1.call-start
  10.0 0.5 all-gather.12.cloned.1.call-update
  10.5 0.0 reduce-scatter.10.cloned.1.call-start
  10.6 31.4 %all-gather.6.cloned.1.call-done = bf16[512,2048]{1,0:T(8,128)(2,1)} async-done(((bf16[512,256]{1,0:T(8,128)(2,1)}), bf16[512,2048]{1,0:T(8,128)(2,1)}) %all-gather.6.cloned.1.call-update) | async-done | bytes 2097168 | tf_op jit(solution)/shard_map/all_gather | solution.py:20
  42.0 83.0 %all-gather.8.cloned.1.call-done = bf16[2048,896]{1,0:T(8,128)(2,1)} async-done(((bf16[64,896]{1,0:T(8,128)(2,1)}), bf16[2048,896]{1,0:T(8,128)(2,1)}) %all-gather.8.cloned.1.call-update) | async-done | bytes 3670032 | tf_op jit(solution)/shard_map/all_gather | solution.py:24
  125.0 7.0 fusion.5
  132.0 0.0 copy-start.5
  132.0 22.2 %all-gather.14.cloned.1.call-done = bf16[512,2048]{1,0:T(8,128)(2,1)} async-done(((bf16[512,256]{1,0:T(8,128)(2,1)}), bf16[512,2048]{1,0:T(8,128)(2,1)}) %all-gather.14.cloned.1.call-update) | async-done | bytes 2097168 | tf_op jit(solution)/shard_map/all_gather | solution.py:19
  154.2 0.0 copy-start.1
  154.2 0.0 copy-start.3
  154.2 0.0 copy-start.7
  154.2 3.8 fusion
  158.1 0.0 copy-done.5
  158.1 0.0 copy-done.1
  158.1 0.0 copy-done.3
  158.1 0.0 copy-done.7
  158.1 4.1 fusion.1
  162.2 6.2 pad_maximum_fusion
  168.4 10.1 %copy.17 = bf16[2048,1792]{1,0:T(8,128)(2,1)} copy(bf16[2048,1792]{0,1:T(8,128)(2,1)} %pad_maximum_fusion) | data formatting | bytes 14680064
  178.5 0.0 copy-start
  178.5 0.0 reduce-scatter.10.cloned.1.call-update
  178.5 0.0 reduce-scatter.12.cloned.1.call-start
  178.5 1.5 copy-done
  180.1 0.2 copy-done.2
  180.3 5.3 fusion.2
  185.6 6.1 copy.19
  191.7 0.0 reduce-scatter.12.cloned.1.call-update
  191.7 0.0 copy-start.4
  191.7 0.2 reduce-scatter.8.cloned.1.call-start
  191.9 45.1 %all-gather.10.cloned.1.call-done = bf16[2048,896]{1,0:T(8,128)(2,1)} async-done(((bf16[64,896]{1,0:T(8,128)(2,1)}), bf16[2048,896]{1,0:T(8,128)(2,1)}) %all-gather.10.cloned.1.call-update) | async-done | bytes 3670032 | tf_op jit(solution)/shard_map/all_gather | solution.py:44
  237.0 0.0 copy-done.6
  237.1 6.5 fusion.14
  243.5 73.4 %all-gather.12.cloned.1.call-done = bf16[2048,896]{1,0:T(8,128)(2,1)} async-done(((bf16[64,896]{1,0:T(8,128)(2,1)}), bf16[2048,896]{1,0:T(8,128)(2,1)}) %all-gather.12.cloned.1.call-update) | async-done | bytes 3670032 | tf_op jit(solution)/shard_map/all_gather | solution.py:45
  317.0 0.0 copy-done.4
  317.0 7.6 add_convert_fusion
  324.5 0.0 reduce-scatter.8.cloned.1.call-update
  324.5 221.4 %reduce-scatter.10.cloned.1.call-done = bf16[64,1792]{1,0:T(8,128)(2,1)} async-done(((bf16[2048,1792]{1,0:T(8,128)(2,1)}), bf16[64,1792]{1,0:T(8,128)(2,1)}) %reduce-scatter.10.cloned.1.call-update) | async-done | bytes 229392
  545.9 1.7 fusion.13
  547.6 222.8 %reduce-scatter.12.cloned.1.call-done = bf16[64,896]{1,0:T(8,128)(2,1)} async-done(((bf16[2048,896]{1,0:T(8,128)(2,1)}), bf16[64,896]{1,0:T(8,128)(2,1)}) %reduce-scatter.12.cloned.1.call-update) | async-done | bytes 114704
  770.4 38.6 %reduce-scatter.8.cloned.1.call-done = bf16[512,256]{1,0:T(8,128)(2,1)} async-done(((bf16[512,2048]{1,0:T(8,128)(2,1)}), bf16[512,256]{1,0:T(8,128)(2,1)}) %reduce-scatter.8.cloned.1.call-update) | async-done | bytes 262160 | tf_op jit(solution)/shard_map/reduce_scatter | solution.py:47
  (2 shorter events, 0.0 us)
Async XLA Ops:
  7.2 34.8 %all-gather.6.cloned.1.call-start = ((), (), s32[]{:S(2)}) async-start(), calls=%async_computation.3 | async-start | bytes 2359296 | tf_op jit(solution)/shard_map/all_gather | solution.py:20
  7.9 117.1 %all-gather.8.cloned.1.call-start = ((), (), s32[]{:S(2)}) async-start(), calls=%async_computation.4 | async-start | bytes 3784704 | tf_op jit(solution)/shard_map/all_gather | solution.py:24
  8.6 145.6 %all-gather.14.cloned.1.call-start = ((), (), s32[]{:S(2)}) async-start(), calls=%async_computation.8 | async-start | bytes 2359296 | tf_op jit(solution)/shard_map/all_gather | solution.py:19
  9.4 227.7 %all-gather.10.cloned.1.call-start = ((), (), s32[]{:S(2)}) async-start(), calls=%async_computation.5 | async-start | bytes 3784704 | tf_op jit(solution)/shard_map/all_gather | solution.py:44
  10.0 307.0 %all-gather.12.cloned.1.call-start = ((), (), s32[]{:S(2)}) async-start(), calls=%async_computation.6 | async-start | bytes 3784704 | tf_op jit(solution)/shard_map/all_gather | solution.py:45
  10.5 535.4 %reduce-scatter.10.cloned.1.call-start = ((), (), s32[]{:S(2)}) async-start(), calls=%async_computation.9 | async-start | bytes 7569408
  132.0 26.1 %copy-start.5 = (bf16[512,896]{1,0:T(8,128)(2,1)}, bf16[512,896]{1,0:T(8,128)(2,1)S(1)}, u32[]{:S(2)}) copy-start(bf16[512,896]{1,0:T(8,128)(2,1)S(1)} %get-tuple-element.14) | copy-start | bytes 2752516
  154.2 3.9 copy-start.1
  154.2 3.9 copy-start.3
  154.2 3.9 copy-start.7
  178.5 1.6 copy-start
  178.5 1.8 copy-start.2
  178.5 592.0 %reduce-scatter.12.cloned.1.call-start = ((), (), s32[]{:S(2)}) async-start(), calls=%async_computation.10 | async-start | bytes 3784704
  191.7 45.4 %copy-start.6 = (bf16[512,896]{1,0:T(8,128)(2,1)S(1)}, bf16[512,896]{1,0:T(8,128)(2,1)}, u32[]{:S(2)}) copy-start(bf16[512,896]{1,0:T(8,128)(2,1)} %copy-done.5) | copy-start | bytes 2752516
  191.7 125.3 %copy-start.4 = (bf16[512,896]{1,0:T(8,128)(2,1)S(1)}, bf16[512,896]{1,0:T(8,128)(2,1)}, u32[]{:S(2)}) copy-start(bf16[512,896]{1,0:T(8,128)(2,1)} %param.9) | copy-start | bytes 2752516
  191.7 617.4 %reduce-scatter.8.cloned.1.call-start = ((), (), s32[]{:S(2)}) async-start(), calls=%async_computation.7 | async-start | bytes 2359296 | tf_op jit(solution)/shard_map/reduce_scatter | solution.py:47
Sparse Core Ops, SparseCore 0:
  9.8 32.1 all-gather.5
  44.6 80.3 all-gather.7
  126.8 27.3 all-gather.13
  156.6 80.3 all-gather.9
  239.5 77.4 all-gather.11
  320.8 225.0 reduce-scatter.9
  550.4 220.0 reduce-scatter.11
  773.6 35.4 reduce-scatter.7
where the time goes:
time: 817 us; the launch traced here: 816 us
  waiting for transfers between devices  741 us (91%)
  matrix products  34.2 us (4%)
  local copies, waits for them, and re-layouts  19.6 us (2%)
  between operations  14.2 us (2%)
    unnamed x10, waiting for transfers between devices  447 us
    all_gather x1, waiting for transfers between devices, body(): lax.all_gather(down_weight, 'row', axis=0, tiled=True)  83 us
    all_gather x1, waiting for transfers between devices, body(): lax.all_gather(up_weight, 'row', axis=0, tiled=True)  73.4 us
    all_gather x1, waiting for transfers between devices, body(): lax.all_gather(gate_weight, 'row', axis=0, tiled=True)  45.1 us
    reduce_scatter x1, waiting for transfers between devices, body(): lax.psum_scatter(part.astype(jnp.bfloat16), 'col', scatter_dimension=1, t...  38.6 us
    all_gather x1, waiting for transfers between devices, body(): lax.all_gather(grad_out, 'col', axis=1, tiled=True)  31.4 us
    all_gather x1, waiting for transfers between devices, body(): lax.all_gather(inputs, 'col', axis=1, tiled=True)  22.2 us
    unnamed x18, local copies, waits for them, and re-layouts  17.9 us
  transfers between devices with their start and end apart: 8, of which 8 were waited for; matrix products, arithmetic and copies ran while one was open for 7% of the time, Pallas kernels for 0%

commit v1 on v0

--- a/solution.py
+++ b/solution.py
@@ -41,9 +41,12 @@
     down_grad = lax.psum_scatter(
         grad_term(full_grads, hidden).astype(jnp.bfloat16), "row", scatter_dimension=0, tiled=True
     )
-    part = against(d_gate, lax.all_gather(gate_weight, "row", axis=0, tiled=True)) + against(
-        d_up, lax.all_gather(up_weight, "row", axis=0, tiled=True)
-    )
+    part = against(
+        d_gate,
+        jnp.concatenate(
+            lax.all_to_all(jnp.stack([gate_weight] * lax.axis_size("row")), "row", 0, 0), axis=0
+        ),
+    ) + against(d_up, lax.all_gather(up_weight, "row", axis=0, tiled=True))
     d_inputs = lax.psum_scatter(part.astype(jnp.bfloat16), "col", scatter_dimension=1, tiled=True)
     paired = lax.psum_scatter(
         jnp.concatenate(

time: 817 us -> 779 us (0.953)
  waiting for transfers between devices: 741 us -> 691 us
  starting transfers between devices: 0.49 us -> 10.9 us
    all_to_all x0 -> x1, waiting for transfers between devices: none -> 88 us  [body(): lax.all_to_all(jnp.stack([gate_weight] * lax.axis_size('row')), 'row', 0, 0)]
    all_gather x1, waiting for transfers between devices: 73.4 us -> 0.01 us  [body(): lax.all_gather(up_weight, 'row', axis=0, tiled=True)]
    all_gather x1 -> x0, waiting for transfers between devices: 45.1 us -> none  [body(): lax.all_gather(gate_weight, 'row', axis=0, tiled=True)]
    unnamed x10 -> x9, waiting for transfers between devices: 447 us -> 428 us
    all_to_all x0 -> x1, starting transfers between devices: none -> 10.5 us  [body(): lax.all_to_all(jnp.stack([gate_weight] * lax.axis_size('row')), 'row', 0, 0)]
    unnamed x18 -> x20, local copies, waits for them, and re-layouts: 17.9 us -> 17.1 us
  transfers between devices with their start and end apart: 8 -> 8, of which waited for: 8 -> 7; matrix products, arithmetic and copies ran while one was open for 7% -> 8% of each run, Pallas kernels for 0% -> 0%
where the time goes in v1:
time: 779 us; the launch traced here: 778 us
  waiting for transfers between devices  691 us (89%)
  matrix products  34.6 us (4%)
  local copies, waits for them, and re-layouts  21.2 us (3%)
  between operations  14.2 us (2%)
  starting transfers between devices  10.9 us (1%)
    unnamed x9, waiting for transfers between devices  428 us
    all_to_all x1, waiting for transfers between devices, body(): lax.all_to_all(jnp.stack([gate_weight] * lax.axis_size('row')), 'row', 0, 0)  88 us
    all_gather x1, waiting for transfers between devices, body(): lax.all_gather(down_weight, 'row', axis=0, tiled=True)  83 us
    reduce_scatter x1, waiting for transfers between devices, body(): lax.psum_scatter(part.astype(jnp.bfloat16), 'col', scatter_dimension=1, t...  38.7 us
    all_gather x1, waiting for transfers between devices, body(): lax.all_gather(grad_out, 'col', axis=1, tiled=True)  32 us
    all_gather x1, waiting for transfers between devices, body(): lax.all_gather(inputs, 'col', axis=1, tiled=True)  22.2 us
    unnamed x20, local copies, waits for them, and re-layouts  17.1 us
  transfers between devices with their start and end apart: 8, of which 7 were waited for; matrix products, arithmetic and copies ran while one was open for 8% of the time, Pallas kernels for 0%

profile of v1, /device:TPU:8, one launch (start us, length us, event | category | flops | bytes accessed | tf_op | source)
XLA Modules:
  0.0 778.5 jit_solution(13302332286418441859)
XLA Ops:
  7.2 0.0 all-gather.5.cloned.1.call-start
  7.2 0.7 all-gather.5.cloned.1.call-update
  7.9 0.0 all-gather.7.cloned.1.call-start
  7.9 0.7 all-gather.7.cloned.1.call-update
  8.6 0.0 all-gather.11.cloned.1.call-start
  8.7 0.7 all-gather.11.cloned.1.call-update
  9.4 0.0 all-gather.9.cloned.1.call-start
  9.4 0.5 all-gather.9.cloned.1.call-update
  10.0 0.0 reduce-scatter.10.cloned.1.call-start
  10.0 32.0 %all-gather.5.cloned.1.call-done = bf16[512,2048]{1,0:T(8,128)(2,1)} async-done(((bf16[512,256]{1,0:T(8,128)(2,1)}), bf16[512,2048]{1,0:T(8,128)(2,1)}) %all-gather.5.cloned.1.call-update) | async-done | bytes 2097168 | tf_op jit(solution)/shard_map/all_gather | solution.py:20
  42.0 83.0 %all-gather.7.cloned.1.call-done = bf16[2048,896]{1,0:T(8,128)(2,1)} async-done(((bf16[64,896]{1,0:T(8,128)(2,1)}), bf16[2048,896]{1,0:T(8,128)(2,1)}) %all-gather.7.cloned.1.call-update) | async-done | bytes 3670032 | tf_op jit(solution)/shard_map/all_gather | solution.py:24
  125.0 7.0 fusion.5
  132.0 0.0 copy-start.6
  132.0 22.2 %all-gather.11.cloned.1.call-done = bf16[512,2048]{1,0:T(8,128)(2,1)} async-done(((bf16[512,256]{1,0:T(8,128)(2,1)}), bf16[512,2048]{1,0:T(8,128)(2,1)}) %all-gather.11.cloned.1.call-update) | async-done | bytes 2097168 | tf_op jit(solution)/shard_map/all_gather | solution.py:19
  154.2 0.0 copy-start.2
  154.2 0.0 copy-start.4
  154.2 0.0 copy-start.8
  154.2 3.8 fusion
  158.1 0.0 copy-done.6
  158.1 0.0 copy-done.2
  158.1 0.0 copy-done.4
  158.1 0.0 copy-done.8
  158.1 4.0 fusion.1
  162.1 6.2 pad_maximum_fusion
  168.3 10.1 %copy.17 = bf16[2048,1792]{1,0:T(8,128)(2,1)} copy(bf16[2048,1792]{0,1:T(8,128)(2,1)} %pad_maximum_fusion) | data formatting | bytes 14680064
  178.4 0.0 copy-start
  178.4 0.0 reduce-scatter.10.cloned.1.call-update
  178.4 0.9 copy-done
  179.3 2.4 stack.2
  181.8 0.0 copy-start.1
  181.8 10.5 %all-to-all-start = ((bf16[32,64,896]{2,1,0:T(8,128)(2,1)}), bf16[32,64,896]{2,1,0:T(8,128)(2,1)}, u32[]{:S(2)}, u32[]{:S(2)}) async-start(bf16[32,64,896]{2,1,0:T(8,128)(2,1)} %stack.2), calls=%async_computation | async-start | bytes 7340032 | tf_op jit(solution)/shard_map/all_to_all | solution.py:47
  192.2 0.0 reduce-scatter.12.cloned.1.call-start
  192.3 0.0 copy-done.1
  192.3 0.0 copy-done.3
  192.3 5.3 fusion.2
  197.6 6.1 copy.19
  203.7 0.0 reduce-scatter.12.cloned.1.call-update
  203.7 0.2 reduce-scatter.8.cloned.1.call-start
  204.0 88.0 %all-to-all-done = bf16[32,64,896]{2,1,0:T(8,128)(2,1)} async-done(((bf16[32,64,896]{2,1,0:T(8,128)(2,1)}), bf16[32,64,896]{2,1,0:T(8,128)(2,1)}, u32[]{:S(2)}, u32[]{:S(2)}) %all-to-all-start) | async-done | bytes 3670048 | tf_op jit(solution)/shard_map/all_to_all | solution.py:47
  291.9 0.0 copy-done.7
  292.0 6.7 fusion.14
  298.6 0.0 copy-done.5
  298.6 7.7 add_convert_fusion
  306.4 0.0 reduce-scatter.8.cloned.1.call-update
  306.4 202.1 %reduce-scatter.10.cloned.1.call-done = bf16[64,1792]{1,0:T(8,128)(2,1)} async-done(((bf16[2048,1792]{1,0:T(8,128)(2,1)}), bf16[64,1792]{1,0:T(8,128)(2,1)}) %reduce-scatter.10.cloned.1.call-update) | async-done | bytes 229392
  508.5 1.7 fusion.13
  510.2 222.8 %reduce-scatter.12.cloned.1.call-done = bf16[64,896]{1,0:T(8,128)(2,1)} async-done(((bf16[2048,896]{1,0:T(8,128)(2,1)}), bf16[64,896]{1,0:T(8,128)(2,1)}) %reduce-scatter.12.cloned.1.call-update) | async-done | bytes 114704
  733.0 38.7 %reduce-scatter.8.cloned.1.call-done = bf16[512,256]{1,0:T(8,128)(2,1)} async-done(((bf16[512,2048]{1,0:T(8,128)(2,1)}), bf16[512,256]{1,0:T(8,128)(2,1)}) %reduce-scatter.8.cloned.1.call-update) | async-done | bytes 262160 | tf_op jit(solution)/shard_map/reduce_scatter | solution.py:50
  (4 shorter events, 0.0 us)
Async XLA Ops:
  7.2 34.8 %all-gather.5.cloned.1.call-start = ((), (), s32[]{:S(2)}) async-start(), calls=%async_computation.4 | async-start | bytes 2359296 | tf_op jit(solution)/shard_map/all_gather | solution.py:20
  7.9 117.1 %all-gather.7.cloned.1.call-start = ((), (), s32[]{:S(2)}) async-start(), calls=%async_computation.5 | async-start | bytes 3784704 | tf_op jit(solution)/shard_map/all_gather | solution.py:24
  8.6 145.6 %all-gather.11.cloned.1.call-start = ((), (), s32[]{:S(2)}) async-start(), calls=%async_computation.8 | async-start | bytes 2359296 | tf_op jit(solution)/shard_map/all_gather | solution.py:19
  9.4 289.3 %all-gather.9.cloned.1.call-start = ((), (), s32[]{:S(2)}) async-start(), calls=%async_computation.6 | async-start | bytes 3784704 | tf_op jit(solution)/shard_map/all_gather | solution.py:49
  10.0 498.6 %reduce-scatter.10.cloned.1.call-start = ((), (), s32[]{:S(2)}) async-start(), calls=%async_computation.9 | async-start | bytes 7569408
  132.0 26.1 %copy-start.6 = (bf16[512,896]{1,0:T(8,128)(2,1)}, bf16[512,896]{1,0:T(8,128)(2,1)S(1)}, u32[]{:S(2)}) copy-start(bf16[512,896]{1,0:T(8,128)(2,1)S(1)} %get-tuple-element.14) | copy-start | bytes 2752516
  154.2 3.9 copy-start.2
  154.2 3.9 copy-start.4
  154.2 3.9 copy-start.8
  178.4 0.9 copy-start
  181.8 10.5 %copy-start.1 = (bf16[512,2048]{1,0:T(8,128)(2,1)S(1)}, bf16[512,2048]{1,0:T(8,128)(2,1)}, u32[]{:S(2)}) copy-start(bf16[512,2048]{1,0:T(8,128)(2,1)} %all-gather.5.cloned.1.call-done) | copy-start | bytes 6291460
  181.8 10.5 %copy-start.3 = (bf16[512,896]{1,0:T(8,128)(2,1)S(1)}, bf16[512,896]{1,0:T(8,128)(2,1)}, u32[]{:S(2)}) copy-start(bf16[512,896]{1,0:T(8,128)(2,1)} %param.10) | copy-start | bytes 2752516
  181.8 110.2 %all-to-all-start = ((bf16[32,64,896]{2,1,0:T(8,128)(2,1)}), bf16[32,64,896]{2,1,0:T(8,128)(2,1)}, u32[]{:S(2)}, u32[]{:S(2)}) async-start(bf16[32,64,896]{2,1,0:T(8,128)(2,1)} %stack.2), calls=%async_computation | async-start | bytes 7340032 | tf_op jit(solution)/shard_map/all_to_all | solution.py:47
  192.2 540.8 %reduce-scatter.12.cloned.1.call-start = ((), (), s32[]{:S(2)}) async-start(), calls=%async_computation.10 | async-start | bytes 3784704
  203.7 88.2 %copy-start.7 = (bf16[512,896]{1,0:T(8,128)(2,1)S(1)}, bf16[512,896]{1,0:T(8,128)(2,1)}, u32[]{:S(2)}) copy-start(bf16[512,896]{1,0:T(8,128)(2,1)} %copy-done.6) | copy-start | bytes 2752516
  203.7 567.9 %reduce-scatter.8.cloned.1.call-start = ((), (), s32[]{:S(2)}) async-start(), calls=%async_computation.7 | async-start | bytes 2359296 | tf_op jit(solution)/shard_map/reduce_scatter | solution.py:50
  291.9 6.7 copy-start.5
Sparse Core Ops, SparseCore 0:
  9.8 32.1 all-gather.4
  44.6 80.3 all-gather.6
  126.8 27.3 all-gather.10
  156.6 124.7 all-gather.8
  285.4 223.1 reduce-scatter.9
  512.8 220.0 reduce-scatter.11
  736.1 35.4 reduce-scatter.7
